TPU v7x, 256 devices: a whole 4x4x8 slice. The times are simulated.
256 devices in a mesh: depth: 2 (over core), tile: 128 (over z, y, x).
Axes of the slice: x: 4, y: 4, z: 8, core: 2. Of those that a mesh axis runs over, the one named last changes fastest.
Arguments:
- transmission: float32 [2, 4, 8192, 2048], P(None, 'depth', 'tile'), may hold values from -1 to 1, as said below
- probe: float32 [2, 128, 128], replicated, may hold values from -4 to 4
- scan_rows: int32 [1024], P('tile'), may hold values from 0 to 8064, as said below
- scan_cols: int32 [1024], P('tile'), may hold values from 0 to 1920
- tile_counts: int32 [128], replicated, may hold values from 1 to 8, as said below
- diffraction: float32 [1024, 128, 128], P('tile'), may hold values from 0 to 2
Outputs:
- object_grad: float32 [2, 4, 8192, 2048], P(None, 'depth', 'tile')
- probe_grad: float32 [2, 128, 128], P(None, 'depth')
Inputs may be any that keep to these rules, and one draw needn't show every extreme that they name: `scan_rows`: slot i's row lies within [t * 64 - 128/2, t * 64 + 64 - 128/2) for t = i // 8, clipped to the specimen; both ends of the specimen are reached. `tile_counts`: some strip has all 8 slots filled and some strip only one. `transmission`: every entry has magnitude between 0.8 and 1.
All inputs are finite; a program needn't handle non-finite values.
Results may differ from a plain program's by a relative error of at most 0.0003.
Values sent between devices are 32-bit elements; how exact they have to be, the bound alone decides.
No kernel may reach another device: no remote copies, remote signals or barrier semaphores. Data moves between devices by JAX's collectives and lax.ppermute only.
A program may use at most 320 MiB of HBM per device.

v0:
```python
import math
import jax
import jax.numpy as jnp
from jax import lax
from jax.sharding import PartitionSpec as P

FRESNEL = 0.5
HIGH = lax.Precision.HIGHEST


def with_halo(value, sides, width):
    for axis, dim in sides:
        size, length = (lax.axis_size(axis), value.shape[dim])
        up = [(i, (i + 1) % size) for i in range(size - 1)]
        down = [(j, i) for i, j in up]
        last = lax.slice_in_dim(value, length - width, length, axis=dim)
        first = lax.slice_in_dim(value, 0, width, axis=dim)
        before = lax.ppermute(last, axis, up)
        after = lax.ppermute(first, axis, down)
        value = jnp.concatenate([before, value, after], axis=dim)
    return value


def shifted(value, axis, by):
    size = lax.axis_size(axis)
    pairs = [(i, i + by) for i in range(size) if 0 <= i + by < size]
    return lax.ppermute(value, axis, pairs)


def dft_tables(size):
    index = jnp.arange(size, dtype=jnp.int32)
    product = index[:, None] * index[None, :] % size
    angle = 2.0 * math.pi / size * product.astype(jnp.float32)
    scale = 1.0 / math.sqrt(size)
    cosine = jnp.cos(angle) * scale
    sine = jnp.sin(angle) * scale
    freq = ((index + size // 2) % size - size // 2).astype(jnp.float32)
    phase = FRESNEL * math.pi / size * (freq[:, None] ** 2 + freq[None, :] ** 2)
    return (cosine, sine, jnp.cos(phase), jnp.sin(phase))


def left_mul(real_m, imag_m, wave):
    wave_re = wave[..., 0, :, :]
    wave_im = wave[..., 1, :, :]

    def prod(m, x):
        return jnp.einsum("ij,...jk->...ik", m, x, precision=HIGH)

    return jnp.stack(
        [
            prod(real_m, wave_re) - prod(imag_m, wave_im),
            prod(real_m, wave_im) + prod(imag_m, wave_re),
        ],
        axis=-3,
    )


def right_mul(wave, real_m, imag_m):
    wave_re = wave[..., 0, :, :]
    wave_im = wave[..., 1, :, :]

    def prod(x, m):
        return jnp.einsum("...ij,jk->...ik", x, m, precision=HIGH)

    return jnp.stack(
        [
            prod(wave_re, real_m) - prod(wave_im, imag_m),
            prod(wave_re, imag_m) + prod(wave_im, real_m),
        ],
        axis=-3,
    )


def transform(wave, cosine, sine, sign):
    imag_m = sign * sine
    return right_mul(left_mul(cosine, imag_m, wave), cosine, imag_m)


def times(first, second):
    a_re, a_im = (first[..., 0, :, :], first[..., 1, :, :])
    b_re, b_im = (second[..., 0, :, :], second[..., 1, :, :])
    return jnp.stack([a_re * b_re - a_im * b_im, a_re * b_im + a_im * b_re], axis=-3)


def conj_times(first, second):
    a_re, a_im = (first[..., 0, :, :], first[..., 1, :, :])
    b_re, b_im = (second[..., 0, :, :], second[..., 1, :, :])
    return jnp.stack([a_re * b_re + a_im * b_im, a_re * b_im - a_im * b_re], axis=-3)


def propagate(wave, tables, adjoint):
    cosine, sine, kern_cos, kern_sin = tables
    spectrum = transform(wave, cosine, sine, -1.0)
    kernel = jnp.stack([kern_cos, kern_sin if adjoint else -kern_sin])
    return transform(times(kernel, spectrum), cosine, sine, 1.0)


def shards(transmission, probe, scan_rows, scan_cols, tile_counts, diffraction):
    size = probe.shape[-1]
    half = size // 2
    group = transmission.shape[1]
    strip = transmission.shape[2]
    slots = scan_rows.shape[0]
    tables = dft_tables(size)
    cosine, sine = (tables[0], tables[1])
    n_depth = lax.axis_size("depth")
    depth_pos = lax.axis_index("depth")
    tile_pos = lax.axis_index("tile")
    first = depth_pos == 0
    last = depth_pos == n_depth - 1
    filled = tile_counts[tile_pos]
    extended = with_halo(transmission, (("tile", 2),), half)
    local_rows = scan_rows - (tile_pos * strip - half)
    batch = 1
    offsets = jnp.arange(batch, dtype=jnp.int32)
    zero_index = jnp.int32(0)

    def cut(row, col):
        return lax.dynamic_slice(
            extended, (zero_index, zero_index, row, col), (2, group, size, size)
        )

    own_bank = jax.vmap(cut)(local_rows, scan_cols)

    def walk(wave, patches, finish):
        inputs = []
        for slice_pos in range(group):
            inputs.append(wave)
            if finish or slice_pos + 1 < group:
                wave = propagate(times(patches[:, :, slice_pos], wave), tables, False)
        return (wave, jnp.stack(inputs, axis=1))

    def seed_of(out_wave, measured):
        far = transform(out_wave, cosine, sine, -1.0)
        intensity = far[:, 0] ** 2 + far[:, 1] ** 2
        return transform((intensity - measured)[:, None] * far, cosine, sine, 1.0)

    grads_start = jnp.zeros(extended.shape, jnp.float32)
    order = jnp.arange(slots, dtype=jnp.int32)
    n_blocks = slots // batch
    count = order.shape[0]
    blocks = count // batch
    segments = n_blocks + n_depth - 1
    wave_shape = (batch, 2, size, size)

    def slot_state(block):
        positions = block * batch + offsets
        valid = (block >= 0) & (block < n_blocks) & (positions < filled)
        start = jnp.clip(block, 0, blocks - 1) * batch
        ids = order[start + offsets]
        return (valid, start, ids)

    saved_start = jnp.zeros((count, 2, size, size), jnp.float32)
    seeds_start = jnp.zeros((count, 2, size, size), jnp.float32)

    def forward_segment(step, state):
        incoming, saved, seeds = state
        valid, start, ids = slot_state(step - depth_pos)
        mask = valid.astype(jnp.float32)[:, None, None, None]
        wave = jnp.where(first, probe[None], incoming) * mask

        def forward_work(args):
            saved_in, seeds_in = args
            out_wave, inputs = walk(wave, jnp.take(own_bank, ids, axis=0), True)
            kept = inputs[:, 0]
            saved_out = lax.dynamic_update_slice_in_dim(saved_in, kept, start, 0)

            def write_seed(buffer):
                measured = jnp.take(diffraction, ids, axis=0)
                return lax.dynamic_update_slice_in_dim(
                    buffer, seed_of(out_wave, measured), start, 0
                )

            def leave_seed(buffer):
                return buffer

            seeds_out = lax.cond(last, write_seed, leave_seed, seeds_in)
            return (out_wave, saved_out, seeds_out)

        def forward_rest(args):
            return (jnp.zeros(wave_shape, jnp.float32), args[0], args[1])

        out_wave, saved, seeds = lax.cond(
            jnp.any(valid), forward_work, forward_rest, (saved, seeds)
        )
        incoming = shifted(out_wave, "depth", 1)
        return (incoming, saved, seeds)

    incoming0 = jnp.zeros(wave_shape, jnp.float32)
    _, saved, seeds = lax.fori_loop(
        0, segments, forward_segment, (incoming0, saved_start, seeds_start)
    )

    def backward_segment(step, state):
        incoming, windows, probe_acc = state
        valid, start, ids = slot_state(step - (n_depth - 1 - depth_pos))
        mask = valid.astype(jnp.float32)[:, None, None, None]
        arriving = (
            jnp.where(last, lax.dynamic_slice_in_dim(seeds, start, batch, 0), incoming) * mask
        )

        def backward_work(args):
            windows_in, probe_in = args
            patches = jnp.take(own_bank, ids, axis=0)
            _, inputs = walk(lax.dynamic_slice_in_dim(saved, start, batch, 0), patches, False)
            flow = arriving
            pieces = [None] * group
            for slice_pos in reversed(range(group)):
                along = propagate(flow, tables, True)
                pieces[slice_pos] = conj_times(inputs[:, slice_pos], along)
                flow = conj_times(patches[:, :, slice_pos], along)
            update = (
                jnp.stack(pieces, axis=2) * valid.astype(jnp.float32)[:, None, None, None, None]
            )
            windows_out = lax.dynamic_update_slice_in_dim(windows_in, update, start, 0)
            probe_out = probe_in + jnp.where(first, jnp.sum(flow * mask, axis=0), 0.0)
            return (flow, windows_out, probe_out)

        def backward_rest(args):
            return (jnp.zeros(wave_shape, jnp.float32), args[0], args[1])

        out_wave, windows, probe_acc = lax.cond(
            jnp.any(valid), backward_work, backward_rest, (windows, probe_acc)
        )
        incoming = shifted(out_wave, "depth", -1)
        return (incoming, windows, probe_acc)

    windows_start = jnp.zeros((count, 2, group, size, size), jnp.float32)
    probe_start = jnp.zeros(probe.shape, jnp.float32)
    _, windows, probe_acc = lax.fori_loop(
        0, segments, backward_segment, (incoming0, windows_start, probe_start)
    )
    windows, probe_acc = (windows, probe_acc)
    weights = jnp.ones((slots,), jnp.float32)

    def place_one(item, total):
        slot_id = order[item]
        place = (zero_index, zero_index, local_rows[slot_id], scan_cols[slot_id])
        current = lax.dynamic_slice(total, place, (2, group, size, size))
        return lax.dynamic_update_slice(total, current + windows[item] * weights[item], place)

    grads = lax.fori_loop(0, order.shape[0], place_one, grads_start)
    rims = jnp.concatenate([grads[:, :, :half], grads[:, :, half + strip :]], axis=2)
    arrived = with_halo(rims, (("tile", 2),), half)
    own = grads[:, :, half : half + strip]
    own = own.at[:, :, :half].add(arrived[:, :, :half])
    own = own.at[:, :, strip - half :].add(arrived[:, :, 3 * half :])
    probe_rows = lax.psum_scatter(probe_acc, "depth", scatter_dimension=1, tiled=True)
    probe_grad = lax.psum(probe_rows, "tile")
    return (own, probe_grad)


def solution(mesh):
    placed = (P(None, "depth", "tile", None), P(), P("tile"), P("tile"), P(), P("tile", None, None))
    return jax.shard_map(
        shards,
        mesh=mesh,
        in_specs=placed,
        out_specs=(P(None, "depth", "tile", None), P(None, "depth", None)),
        check_vma=False,
    )
```

profile of v0, /device:TPU:2, one launch (start us, length us, event | category | flops | bytes accessed | tf_op | source)
XLA Modules:
  0.0 889.9 jit_solution(7273562203496722747)
XLA Ops:
  7.2 3.4 collective-permute-start.2
  10.6 2.6 collective-permute-start.3
  15.8 40.8 %collective-permute-done.2 = f32[2,2,64,2048]{3,2,1,0:T(8,128)S(1)} collective-permute-done((f32[2,2,64,2048]{3,2,1,0:T(8,128)}, f32[2,2,64,2048]{3,2,1,0:T(8,128)S(1)}, u32[]{:S(2)}, u32[]{:S(2)}) %collective-permute-start.2) | collective-permute-done | bytes 2097184 | tf_op jit(solution)/shard_map/ppermute | solution.py:18
  56.7 3.2 collective-permute-done.3
  59.9 5.7 pad_maximum_fusion.2
  65.8 24.3 %while.68 = (s32[]{:T(128)}, f32[2,2,192,2048]{3,2,1,0:T(8,128)}, s32[8,4]{0,1:T(4,128)S(1)}, f32[8,2,2,128,128]{4,3,1,2,0:T(8,128)S(1)}, s32[]{:T(128)}) while((s32[]{:T(128)}, f32[2,2,192,2048]{3,2,1,0:T(8,128)}, s32[8,4]{0,1:T(4,128)S(1)}, f32[8,2,2,128,128]{4,3,1,2,0:T(8,128)S(1)}, s32[]{:T(128)}) %tuple.373), condition=%wide.while_cond.6, body=%wide.while_body.6.sunk | while | flops 2 | bytes 525937 | solution.py:119
  66.5 2.4 copy_dynamic-update-slice_fusion.2
  69.5 2.4 copy_dynamic-update-slice_fusion.2
  72.6 2.4 copy_dynamic-update-slice_fusion.2
  75.6 2.4 copy_dynamic-update-slice_fusion.2
  78.7 2.4 copy_dynamic-update-slice_fusion.2
  81.7 2.4 copy_dynamic-update-slice_fusion.2
  84.8 2.4 copy_dynamic-update-slice_fusion.2
  87.8 2.4 copy_dynamic-update-slice_fusion.2
  92.4 91.4 %while.69 = (s32[]{:T(128)}, f32[1,2,128,128]{3,2,1,0:T(8,128)S(1)}, f32[8,2,128,128]{3,2,1,0:T(8,128)}, f32[8,2,128,128]{3,2,1,0:T(8,128)}, s32[]{:T(128)}, /*i...) while((s32[]{:T(128)}, ...), condition=%wide.region_5.7_spmd.clone.clone.clone, body=%wide.region_0.6_spmd.clone.clone.clone.sunk | while | flops 1209614336 | bytes 16059241 | solution.py:190
  93.1 13.6 %conditional.12 = (f32[1,2,128,128]{3,2,1,0:T(8,128)S(1)}, f32[8,2,128,128]{3,2,1,0:T(8,128)}, f32[8,2,128,128]{3,2,1,0:T(8,128)}) conditional(s32[]{:T(128)} %bitcast.558, (f32[8,2,128,128]{3,2,1,0:T(8,128)}, f32[8,2,128,128]{3,2,1,0:T(8,128)}) %tuple.363, (s32[]{:T(128)}, s32[8]{0:T(128)S(1)}, f32[8,2,2,128,128]{4,3,1,2,0:T(8,128)S(1)}, ...), branch_computations={%region_1.1_spmd, %region_2.5_spmd.clone} | conditional | flops 1209352192 | bytes 15337401 | solution.py:183
  109.6 13.6 %conditional.12 = (f32[1,2,128,128]{3,2,1,0:T(8,128)S(1)}, f32[8,2,128,128]{3,2,1,0:T(8,128)}, f32[8,2,128,128]{3,2,1,0:T(8,128)}) conditional(s32[]{:T(128)} %bitcast.558, (f32[8,2,128,128]{3,2,1,0:T(8,128)}, f32[8,2,128,128]{3,2,1,0:T(8,128)}) %tuple.363, (s32[]{:T(128)}, s32[8]{0:T(128)S(1)}, f32[8,2,2,128,128]{4,3,1,2,0:T(8,128)S(1)}, ...), branch_computations={%region_1.1_spmd, %region_2.5_spmd.clone} | conditional | flops 1209352192 | bytes 15337401 | solution.py:183
  123.2 10.3 %collective-permute-start = (f32[1,2,128,128]{3,2,1,0:T(8,128)S(1)}, f32[1,2,128,128]{3,2,1,0:T(8,128)S(1)}, u32[]{:S(2)}, u32[]{:S(2)}) collective-permute-start(f32[1,2,128,128]{3,2,1,0:T(8,128)S(1)} %get-tuple-element.2643), channel_id=1, source_target_pairs={{0,128},{1,129},{2,130},{3,131},{4,132},{5,133},{6,134},{7,135},{8... | collective-permute-start | bytes 393224 | tf_op jit(solution)/shard_map/while/body/eval_jaxpr/ppermute | solution.py:27
  135.2 23.9 %collective-permute-start = (f32[1,2,128,128]{3,2,1,0:T(8,128)S(1)}, f32[1,2,128,128]{3,2,1,0:T(8,128)S(1)}, u32[]{:S(2)}, u32[]{:S(2)}) collective-permute-start(f32[1,2,128,128]{3,2,1,0:T(8,128)S(1)} %get-tuple-element.2643), channel_id=1, source_target_pairs={{0,128},{1,129},{2,130},{3,131},{4,132},{5,133},{6,134},{7,135},{8... | collective-permute-start | bytes 393224 | tf_op jit(solution)/shard_map/while/body/eval_jaxpr/ppermute | solution.py:27
  160.7 2.3 collective-permute-start
  164.7 2.3 collective-permute-start
  168.6 2.3 collective-permute-start
  172.6 2.3 collective-permute-start
  176.6 2.3 collective-permute-start
  180.5 2.3 collective-permute-start
  185.4 94.9 %while.70 = (s32[]{:T(128)}, f32[1,2,128,128]{3,2,1,0:T(8,128)S(1)}, f32[8,2,2,128,128]{4,3,1,2,0:T(8,128)}, f32[2,128,128]{2,1,0:T(8,128)S(1)}, s32[]{:T(128)},...) while((s32[]{:T(128)}, ...), condition=%wide.region_9.11_spmd.clone.clone.clone, body=%wide.region_6.10_spmd.clone.clone.clone.sunk | while | flops 1210138624 | bytes 17565816 | solution.py:230
  187.6 21.1 %collective-permute-done.1 = f32[1,2,128,128]{3,2,1,0:T(8,128)S(1)} collective-permute-done((f32[1,2,128,128]{3,2,1,0:T(8,128)S(1)}, f32[1,2,128,128]{3,2,1,0:T(8,128)S(1)}, u32[]{:S(2)}, u32[]{:S(2)}) %collective-permute-start.1) | collective-permute-done | bytes 131104 | tf_op jit(solution)/shard_map/while/body/eval_jaxpr/ppermute | solution.py:27
  209.3 20.0 %conditional.13 = (f32[1,2,128,128]{3,2,1,0:T(8,128)S(1)}, f32[8,2,2,128,128]{4,3,1,2,0:T(8,128)}, f32[2,128,128]{2,1,0:T(8,128)S(1)}) conditional(s32[]{:T(128)} %bitcast.561, (f32[8,2,2,128,128]{4,3,1,2,0:T(8,128)}, f32[2,128,128]{2,1,0:T(8,128)S(1)}) %tuple.367, (s32[]{:T(128)}, s32[8]{0:T(128)S(1)}, f32[8,2,2,128,128]{4,3,1,2,0:T(8,128)S(1)}, ...), branch_computations={%region_7.8_spmd, %region_8.9_spmd.clone} | conditional | flops 1209876480 | bytes 16843968 | solution.py:222
  230.6 1.9 collective-permute-done.1
  233.2 20.0 %conditional.13 = (f32[1,2,128,128]{3,2,1,0:T(8,128)S(1)}, f32[8,2,2,128,128]{4,3,1,2,0:T(8,128)}, f32[2,128,128]{2,1,0:T(8,128)S(1)}) conditional(s32[]{:T(128)} %bitcast.561, (f32[8,2,2,128,128]{4,3,1,2,0:T(8,128)}, f32[2,128,128]{2,1,0:T(8,128)S(1)}) %tuple.367, (s32[]{:T(128)}, s32[8]{0:T(128)S(1)}, f32[8,2,2,128,128]{4,3,1,2,0:T(8,128)S(1)}, ...), branch_computations={%region_7.8_spmd, %region_8.9_spmd.clone} | conditional | flops 1209876480 | bytes 16843968 | solution.py:222
  254.5 1.9 collective-permute-done.1
  258.5 1.9 collective-permute-done.1
  262.4 1.9 collective-permute-done.1
  280.2 3.4 broadcast_in_dim.96
  283.7 103.7 %while.67 = (s32[]{:T(128)}, f32[2,2,192,2048]{3,2,1,0:T(8,128)}, s32[8]{0:T(128)S(1)}, s32[8]{0:T(128)S(1)}, s32[8]{0:T(128)S(1)}, /*index=5*/f32[8,2,2,128,128...) while((s32[]{:T(128)}, f32[2,2,192,2048]{3,2,1,0:T(8,128)}, ...), condition=%wide.region_11.13_spmd, body=%wide.region_10.12_spmd.sunk | while | flops 65547 | bytes 1311491 | solution.py:242
  292.5 4.0 dynamic_update_slice.29
  305.4 4.1 dynamic_update_slice.29
  318.3 4.1 dynamic_update_slice.29
  331.3 4.0 dynamic_update_slice.29
  344.1 4.2 dynamic_update_slice.29
  357.1 4.1 dynamic_update_slice.29
  370.0 4.2 dynamic_update_slice.29
  383.1 4.3 dynamic_update_slice.29
  387.4 4.8 fusion.137
  392.2 86.4 %collective-permute-start.4 = (f32[2,2,64,2048]{3,2,1,0:T(8,128)}, f32[2,2,64,2048]{3,2,1,0:T(8,128)S(1)}, u32[]{:S(2)}, u32[]{:S(2)}) collective-permute-start(f32[2,2,64,2048]{3,2,1,0:T(8,128)} %get-tuple-element.2429), channel_id=1, source_target_pairs={{0,1},{1,2},{2,3},{3,4},{4,5},{5,6},{6,7},{7,8},{8,9},{9,10},{10,1... | collective-permute-start | bytes 6291464 | tf_op jit(solution)/shard_map/ppermute | solution.py:18
  480.6 181.8 %reduce-scatter.2.cloned.1.call-done = f32[2,64,128]{2,1,0:T(8,128)} async-done(((f32[2,128,128]{2,1,0:T(8,128)}), f32[2,64,128]{2,1,0:T(8,128)}) %reduce-scatter.2.cloned.1.call-update) | async-done | bytes 65552 | tf_op jit(solution)/shard_map/reduce_scatter | solution.py:248
  662.4 4.2 add_add_fusion
  666.6 215.0 %all-reduce.2.cloned.1.call-done = f32[2,64,128]{2,1,0:T(8,128)} async-done(((f32[2,64,128]{2,1,0:T(8,128)}), f32[2,64,128]{2,1,0:T(8,128)}) %all-reduce.2.cloned.1.call-update) | async-done | bytes 65552 | tf_op jit(solution)/shard_map/psum | solution.py:249
  (384 shorter events, 131.3 us)
Async XLA Ops:
  7.2 655.2 %reduce-scatter.2.cloned.1.call-start = ((), (), s32[]{:S(2)}) async-start(), calls=%async_computation.1 | async-start | bytes 196608 | tf_op jit(solution)/shard_map/reduce_scatter | solution.py:248
  7.2 49.5 %collective-permute-start.2 = (f32[2,2,64,2048]{3,2,1,0:T(8,128)}, f32[2,2,64,2048]{3,2,1,0:T(8,128)S(1)}, u32[]{:S(2)}, u32[]{:S(2)}) collective-permute-start(f32[2,2,64,2048]{3,2,1,0:T(8,128)} %param.28), channel_id=1, source_target_pairs={{0,1},{1,2},{2,3},{3,4},{4,5},{5,6},{6,7},{7,8},{8,9},{9,10},{10,1... | collective-permute-start | bytes 6291464 | tf_op jit(solution)/shard_map/ppermute | solution.py:18
  10.6 49.3 %collective-permute-start.3 = (f32[2,2,64,2048]{3,2,1,0:T(8,128)}, f32[2,2,64,2048]{3,2,1,0:T(8,128)}, u32[]{:S(2)}, u32[]{:S(2)}) collective-permute-start(f32[2,2,64,2048]{3,2,1,0:T(8,128)} %param.28), channel_id=1, source_target_pairs={{1,0},{2,1},{3,2},{4,3},{5,4},{6,5},{7,6},{8,7},{9,8},{10,9},{11,1... | collective-permute-start | bytes 6291464 | tf_op jit(solution)/shard_map/ppermute | solution.py:19
  65.8 26.6 %copy-start.1 = (f32[2,128,128]{2,1,0:T(8,128)S(1)}, f32[2,128,128]{2,1,0:T(8,128)}, u32[]{:S(2)}) copy-start(f32[2,128,128]{2,1,0:T(8,128)} %param.29) | copy-start | bytes 393220
  106.7 2.3 collective-permute-start
  123.2 11.3 %collective-permute-start = (f32[1,2,128,128]{3,2,1,0:T(8,128)S(1)}, f32[1,2,128,128]{3,2,1,0:T(8,128)S(1)}, u32[]{:S(2)}, u32[]{:S(2)}) collective-permute-start(f32[1,2,128,128]{3,2,1,0:T(8,128)S(1)} %get-tuple-element.2643), channel_id=1, source_target_pairs={{0,128},{1,129},{2,130},{3,131},{4,132},{5,133},{6,134},{7,135},{8... | collective-permute-start | bytes 393224 | tf_op jit(solution)/shard_map/while/body/eval_jaxpr/ppermute | solution.py:27
  135.2 24.8 %collective-permute-start = (f32[1,2,128,128]{3,2,1,0:T(8,128)S(1)}, f32[1,2,128,128]{3,2,1,0:T(8,128)S(1)}, u32[]{:S(2)}, u32[]{:S(2)}) collective-permute-start(f32[1,2,128,128]{3,2,1,0:T(8,128)S(1)} %get-tuple-element.2643), channel_id=1, source_target_pairs={{0,128},{1,129},{2,130},{3,131},{4,132},{5,133},{6,134},{7,135},{8... | collective-permute-start | bytes 393224 | tf_op jit(solution)/shard_map/while/body/eval_jaxpr/ppermute | solution.py:27
  160.7 3.2 collective-permute-start
  164.7 3.2 collective-permute-start
  168.6 3.2 collective-permute-start
  172.6 3.2 collective-permute-start
  176.6 3.2 collective-permute-start
  180.5 3.2 collective-permute-start
  186.3 22.4 %collective-permute-start.1 = (f32[1,2,128,128]{3,2,1,0:T(8,128)S(1)}, f32[1,2,128,128]{3,2,1,0:T(8,128)S(1)}, u32[]{:S(2)}, u32[]{:S(2)}) collective-permute-start(f32[1,2,128,128]{3,2,1,0:T(8,128)S(1)} %get-tuple-element.2660), channel_id=1, source_target_pairs={{128,0},{129,1},{130,2},{131,3},{132,4},{133,5},{134,6},{135,7},{1... | collective-permute-start | bytes 393224 | tf_op jit(solution)/shard_map/while/body/eval_jaxpr/ppermute | solution.py:27
  229.3 3.2 collective-permute-start.1
  253.2 3.2 collective-permute-start.1
  257.2 3.2 collective-permute-start.1
  261.1 3.2 collective-permute-start.1
  265.1 3.2 collective-permute-start.1
  269.1 3.2 collective-permute-start.1
  273.0 3.2 collective-permute-start.1
  277.0 3.2 collective-permute-start.1
  280.2 3.4 copy-start
  280.2 3.4 copy-start.2
  392.2 270.3 %collective-permute-start.4 = (f32[2,2,64,2048]{3,2,1,0:T(8,128)}, f32[2,2,64,2048]{3,2,1,0:T(8,128)S(1)}, u32[]{:S(2)}, u32[]{:S(2)}) collective-permute-start(f32[2,2,64,2048]{3,2,1,0:T(8,128)} %get-tuple-element.2429), channel_id=1, source_target_pairs={{0,1},{1,2},{2,3},{3,4},{4,5},{5,6},{6,7},{7,8},{8,9},{9,10},{10,1... | collective-permute-start | bytes 6291464 | tf_op jit(solution)/shard_map/ppermute | solution.py:18
  478.6 183.9 %collective-permute-start.5 = (f32[2,2,64,2048]{3,2,1,0:T(8,128)}, f32[2,2,64,2048]{3,2,1,0:T(8,128)}, u32[]{:S(2)}, u32[]{:S(2)}) collective-permute-start(f32[2,2,64,2048]{3,2,1,0:T(8,128)} %get-tuple-element.2430), channel_id=1, source_target_pairs={{1,0},{2,1},{3,2},{4,3},{5,4},{6,5},{7,6},{8,7},{9,8},{10,9},{11,1... | collective-permute-start | bytes 6291464 | tf_op jit(solution)/shard_map/ppermute | solution.py:19
  480.5 401.1 %all-reduce.2.cloned.1.call-start = ((), (), s32[]{:S(2)}) async-start(), calls=%async_computation.2 | async-start | bytes 131072 | tf_op jit(solution)/shard_map/psum | solution.py:249
Sparse Core Ops, SparseCore 0:
  480.6 181.7 reduce-scatter.1
  667.8 213.7 all-reduce.1
where the time goes:
time: 894 us; the launch traced here: 890 us
  waiting for transfers between devices  486 us (54%)
  starting transfers between devices  155 us (17%)
  local copies, waits for them, and re-layouts  91.8 us (10%)
  loops' own time  65.1 us (7%)
  matrix products  47.9 us (5%)
  other arithmetic  29.7 us (3%)
  between operations  14.2 us (2%)
    psum x1, waiting for transfers between devices, shards(): probe_grad = lax.psum(probe_rows, 'tile')  215 us
    reduce_scatter x1, waiting for transfers between devices, shards(): lax.psum_scatter(probe_acc, 'depth', scatter_dimension=1, tiled=True)  182 us
    ppermute x2, starting transfers between devices, with_halo(): before = lax.ppermute(last, axis, up)  89.8 us
    ppermute x18, starting transfers between devices, shifted(): return lax.ppermute(value, axis, pairs)  60.8 us
    ppermute x18, waiting for transfers between devices, shifted(): return lax.ppermute(value, axis, pairs)  45.2 us
    another operation x1, loops' own time, shards(): grads = lax.fori_loop(0, order.shape[0], place_one, grads_start)  44.9 us
    ppermute x2, waiting for transfers between devices, with_halo(): before = lax.ppermute(last, axis, up)  40.8 us
    dynamic_update_slice x8, local copies, waits for them, and re-layouts, place_one(): lax.dynamic_update_slice(total, current + windows[item] * weights[item],...  33 us
  transfers between devices with their start and end apart: 24, of which 22 were waited for; matrix products, arithmetic and copies ran while one was open for 1% of the time, Pallas kernels for 0%

commit v1 on v0

--- a/solution.py
+++ b/solution.py
@@ -96,6 +96,11 @@
 
 
 def shards(transmission, probe, scan_rows, scan_cols, tile_counts, diffraction):
+
+    def obtain_the_patch(content):
+        step_out = lax.all_gather(content, "tile").sum(axis=0)
+        return step_out
+
     size = probe.shape[-1]
     half = size // 2
     group = transmission.shape[1]
@@ -246,7 +251,7 @@
     own = own.at[:, :, :half].add(arrived[:, :, :half])
     own = own.at[:, :, strip - half :].add(arrived[:, :, 3 * half :])
     probe_rows = lax.psum_scatter(probe_acc, "depth", scatter_dimension=1, tiled=True)
-    probe_grad = lax.psum(probe_rows, "tile")
+    probe_grad = obtain_the_patch(probe_rows)
     return (own, probe_grad)
 
 

time: 894 us -> 735 us (0.82); the launches traced: 890 us -> 721 us
  waiting for transfers between devices: 486 us -> 397 us
  starting transfers between devices: 155 us -> 72.8 us
    psum x1 -> x0, waiting for transfers between devices: 215 us -> none  [shards(): probe_grad = lax.psum(probe_rows, 'tile')]
    ppermute x2, starting transfers between devices: 89.8 us -> 7.15 us  [with_halo(): before = lax.ppermute(last, axis, up)]
    reduce_scatter x1, waiting for transfers between devices: 182 us -> 260 us  [shards(): lax.psum_scatter(probe_acc, 'depth', scatter_dimension=1, tiled=True)]
    ppermute x2, waiting for transfers between devices: 40.8 us -> 86.6 us  [with_halo(): before = lax.ppermute(last, axis, up)]
  transfers between devices with their start and end apart: 24 -> 24, of which waited for: 22 -> 23; matrix products, arithmetic and copies ran while one was open for 1% -> 10% of each run, Pallas kernels for 0% -> 0%
where the time goes in v1:
time: 735 us; the launch traced here: 721 us
  waiting for transfers between devices  397 us (54%)
  local copies, waits for them, and re-layouts  87.8 us (12%)
  starting transfers between devices  72.8 us (10%)
  loops' own time  68.4 us (9%)
  matrix products  47.9 us (7%)
  other arithmetic  33.5 us (5%)
  between operations  14.2 us (2%)
    reduce_scatter x1, waiting for transfers between devices, shards(): lax.psum_scatter(probe_acc, 'depth', scatter_dimension=1, tiled=True)  260 us
    ppermute x2, waiting for transfers between devices, with_halo(): before = lax.ppermute(last, axis, up)  86.6 us
    ppermute x18, starting transfers between devices, shifted(): return lax.ppermute(value, axis, pairs)  60.8 us
    another operation x1, loops' own time, shards(): grads = lax.fori_loop(0, order.shape[0], place_one, grads_start)  45.9 us
    ppermute x18, waiting for transfers between devices, shifted(): return lax.ppermute(value, axis, pairs)  45.2 us
    dynamic_update_slice x8, local copies, waits for them, and re-layouts, place_one(): lax.dynamic_update_slice(total, current + windows[item] * weights[item],...  32.9 us
    dot_general x80, matrix products, prod(): return jnp.einsum('...ij,jk->...ik', x, m, precision=HIGH)  25.1 us
    gather x24, local copies, waits for them, and re-layouts  24.2 us
  transfers between devices with their start and end apart: 24, of which 23 were waited for; matrix products, arithmetic and copies ran while one was open for 10% of the time, Pallas kernels for 0%

profile of v1, /device:TPU:2, one launch (start us, length us, event | category | flops | bytes accessed | tf_op | source)
XLA Modules:
  0.0 721.1 jit_solution(10650165308768826969)
XLA Ops:
  7.2 3.4 collective-permute-start.2
  10.6 2.6 collective-permute-start.3
  15.9 40.7 %collective-permute-done.2 = f32[2,2,64,2048]{3,2,1,0:T(8,128)S(1)} collective-permute-done((f32[2,2,64,2048]{3,2,1,0:T(8,128)}, f32[2,2,64,2048]{3,2,1,0:T(8,128)S(1)}, u32[]{:S(2)}, u32[]{:S(2)}) %collective-permute-start.2) | collective-permute-done | bytes 2097184 | tf_op jit(solution)/shard_map/ppermute | solution.py:18
  56.7 3.2 collective-permute-done.3
  59.9 5.7 pad_maximum_fusion.2
  65.8 24.3 %while.68 = (s32[]{:T(128)}, f32[2,2,192,2048]{3,2,1,0:T(8,128)}, s32[8,4]{0,1:T(4,128)S(1)}, f32[8,2,2,128,128]{4,3,1,2,0:T(8,128)S(1)}, s32[]{:T(128)}) while((s32[]{:T(128)}, f32[2,2,192,2048]{3,2,1,0:T(8,128)}, s32[8,4]{0,1:T(4,128)S(1)}, f32[8,2,2,128,128]{4,3,1,2,0:T(8,128)S(1)}, s32[]{:T(128)}) %tuple.377), condition=%wide.while_cond.6, body=%wide.while_body.6.sunk | while | flops 2 | bytes 525937 | solution.py:124
  66.5 2.4 copy_dynamic-update-slice_fusion.2
  69.5 2.4 copy_dynamic-update-slice_fusion.2
  72.6 2.4 copy_dynamic-update-slice_fusion.2
  75.6 2.4 copy_dynamic-update-slice_fusion.2
  78.7 2.4 copy_dynamic-update-slice_fusion.2
  81.7 2.4 copy_dynamic-update-slice_fusion.2
  84.8 2.4 copy_dynamic-update-slice_fusion.2
  87.8 2.4 copy_dynamic-update-slice_fusion.2
  92.4 92.6 %while.69 = (s32[]{:T(128)}, f32[1,2,128,128]{3,2,1,0:T(8,128)S(1)}, f32[8,2,128,128]{3,2,1,0:T(8,128)}, f32[8,2,128,128]{3,2,1,0:T(8,128)}, s32[]{:T(128)}, /*i...) while((s32[]{:T(128)}, ...), condition=%wide.region_5.7_spmd.clone.clone.clone, body=%wide.region_0.6_spmd.clone.clone.clone.sunk | while | flops 1209614336 | bytes 16059241 | solution.py:195
  93.2 13.6 %conditional.12 = (f32[1,2,128,128]{3,2,1,0:T(8,128)S(1)}, f32[8,2,128,128]{3,2,1,0:T(8,128)}, f32[8,2,128,128]{3,2,1,0:T(8,128)}) conditional(s32[]{:T(128)} %bitcast.559, (f32[8,2,128,128]{3,2,1,0:T(8,128)}, f32[8,2,128,128]{3,2,1,0:T(8,128)}) %tuple.367, (s32[]{:T(128)}, s32[8]{0:T(128)S(1)}, f32[8,2,2,128,128]{4,3,1,2,0:T(8,128)S(1)}, ...), branch_computations={%region_1.1_spmd, %region_2.5_spmd.clone} | conditional | flops 1209352192 | bytes 15337401 | solution.py:188
  109.9 13.6 %conditional.12 = (f32[1,2,128,128]{3,2,1,0:T(8,128)S(1)}, f32[8,2,128,128]{3,2,1,0:T(8,128)}, f32[8,2,128,128]{3,2,1,0:T(8,128)}) conditional(s32[]{:T(128)} %bitcast.559, (f32[8,2,128,128]{3,2,1,0:T(8,128)}, f32[8,2,128,128]{3,2,1,0:T(8,128)}) %tuple.367, (s32[]{:T(128)}, s32[8]{0:T(128)S(1)}, f32[8,2,2,128,128]{4,3,1,2,0:T(8,128)S(1)}, ...), branch_computations={%region_1.1_spmd, %region_2.5_spmd.clone} | conditional | flops 1209352192 | bytes 15337401 | solution.py:188
  123.4 10.3 %collective-permute-start = (f32[1,2,128,128]{3,2,1,0:T(8,128)S(1)}, f32[1,2,128,128]{3,2,1,0:T(8,128)S(1)}, u32[]{:S(2)}, u32[]{:S(2)}) collective-permute-start(f32[1,2,128,128]{3,2,1,0:T(8,128)S(1)} %get-tuple-element.2677), channel_id=1, source_target_pairs={{0,128},{1,129},{2,130},{3,131},{4,132},{5,133},{6,134},{7,135},{8... | collective-permute-start | bytes 393224 | tf_op jit(solution)/shard_map/while/body/eval_jaxpr/ppermute | solution.py:27
  135.6 23.9 %collective-permute-start = (f32[1,2,128,128]{3,2,1,0:T(8,128)S(1)}, f32[1,2,128,128]{3,2,1,0:T(8,128)S(1)}, u32[]{:S(2)}, u32[]{:S(2)}) collective-permute-start(f32[1,2,128,128]{3,2,1,0:T(8,128)S(1)} %get-tuple-element.2677), channel_id=1, source_target_pairs={{0,128},{1,129},{2,130},{3,131},{4,132},{5,133},{6,134},{7,135},{8... | collective-permute-start | bytes 393224 | tf_op jit(solution)/shard_map/while/body/eval_jaxpr/ppermute | solution.py:27
  161.3 2.3 collective-permute-start
  165.4 2.3 collective-permute-start
  169.4 2.3 collective-permute-start
  173.5 2.3 collective-permute-start
  177.6 2.3 collective-permute-start
  181.7 2.3 collective-permute-start
  186.6 96.0 %while.70 = (s32[]{:T(128)}, f32[1,2,128,128]{3,2,1,0:T(8,128)S(1)}, f32[8,2,2,128,128]{4,3,1,2,0:T(8,128)}, f32[2,128,128]{2,1,0:T(8,128)S(1)}, s32[]{:T(128)},...) while((s32[]{:T(128)}, ...), condition=%wide.region_9.11_spmd.clone.clone.clone, body=%wide.region_6.10_spmd.clone.clone.clone.sunk | while | flops 1210138624 | bytes 17565816 | solution.py:235
  188.9 21.1 %collective-permute-done.1 = f32[1,2,128,128]{3,2,1,0:T(8,128)S(1)} collective-permute-done((f32[1,2,128,128]{3,2,1,0:T(8,128)S(1)}, f32[1,2,128,128]{3,2,1,0:T(8,128)S(1)}, u32[]{:S(2)}, u32[]{:S(2)}) %collective-permute-start.1) | collective-permute-done | bytes 131104 | tf_op jit(solution)/shard_map/while/body/eval_jaxpr/ppermute | solution.py:27
  210.8 20.0 %conditional.13 = (f32[1,2,128,128]{3,2,1,0:T(8,128)S(1)}, f32[8,2,2,128,128]{4,3,1,2,0:T(8,128)}, f32[2,128,128]{2,1,0:T(8,128)S(1)}) conditional(s32[]{:T(128)} %bitcast.562, (f32[8,2,2,128,128]{4,3,1,2,0:T(8,128)}, f32[2,128,128]{2,1,0:T(8,128)S(1)}) %tuple.371, (s32[]{:T(128)}, s32[8]{0:T(128)S(1)}, f32[8,2,2,128,128]{4,3,1,2,0:T(8,128)S(1)}, ...), branch_computations={%region_7.8_spmd, %region_8.9_spmd.clone} | conditional | flops 1209876480 | bytes 16843968 | solution.py:227
  232.1 1.9 collective-permute-done.1
  234.8 20.0 %conditional.13 = (f32[1,2,128,128]{3,2,1,0:T(8,128)S(1)}, f32[8,2,2,128,128]{4,3,1,2,0:T(8,128)}, f32[2,128,128]{2,1,0:T(8,128)S(1)}) conditional(s32[]{:T(128)} %bitcast.562, (f32[8,2,2,128,128]{4,3,1,2,0:T(8,128)}, f32[2,128,128]{2,1,0:T(8,128)S(1)}) %tuple.371, (s32[]{:T(128)}, s32[8]{0:T(128)S(1)}, f32[8,2,2,128,128]{4,3,1,2,0:T(8,128)S(1)}, ...), branch_computations={%region_7.8_spmd, %region_8.9_spmd.clone} | conditional | flops 1209876480 | bytes 16843968 | solution.py:227
  256.1 1.9 collective-permute-done.1
  283.3 259.7 %reduce-scatter.2.cloned.1.call-done = f32[2,64,128]{2,1,0:T(8,128)} async-done(((f32[2,128,128]{2,1,0:T(8,128)}), f32[2,64,128]{2,1,0:T(8,128)}) %reduce-scatter.2.cloned.1.call-update) | async-done | bytes 65552 | tf_op jit(solution)/shard_map/reduce_scatter | solution.py:253
  543.1 3.5 broadcast_in_dim.96
  546.6 103.7 %while.67 = (s32[]{:T(128)}, f32[2,2,192,2048]{3,2,1,0:T(8,128)}, s32[8]{0:T(128)S(1)}, s32[8]{0:T(128)S(1)}, s32[8]{0:T(128)S(1)}, /*index=5*/f32[8,2,2,128,128...) while((s32[]{:T(128)}, f32[2,2,192,2048]{3,2,1,0:T(8,128)}, ...), condition=%wide.region_11.13_spmd, body=%wide.region_10.12_spmd.sunk | while | flops 65547 | bytes 1311491 | solution.py:247
  555.4 4.0 dynamic_update_slice.29
  568.2 4.0 dynamic_update_slice.29
  581.1 4.2 dynamic_update_slice.29
  594.1 4.0 dynamic_update_slice.29
  607.0 4.2 dynamic_update_slice.29
  620.0 4.0 dynamic_update_slice.29
  632.9 4.3 dynamic_update_slice.29
  646.0 4.2 dynamic_update_slice.29
  650.3 2.5 fusion.137
  652.8 3.7 collective-permute-start.4
  656.5 2.2 collective-permute-start.5
  658.8 45.8 %collective-permute-done.4 = f32[2,2,64,2048]{3,2,1,0:T(8,128)S(1)} collective-permute-done((f32[2,2,64,2048]{3,2,1,0:T(8,128)S(1)}, f32[2,2,64,2048]{3,2,1,0:T(8,128)S(1)}, u32[]{:S(2)}, u32[]{:S(2)}) %collective-permute-start.4) | collective-permute-done | bytes 2097184 | tf_op jit(solution)/shard_map/ppermute | solution.py:18
  706.4 3.4 add_add_fusion
  709.8 4.5 reduce_sum.9
  (384 shorter events, 133.4 us)
Async XLA Ops:
  7.2 535.9 %reduce-scatter.2.cloned.1.call-start = ((), (), s32[]{:S(2)}) async-start(), calls=%async_computation.1 | async-start | bytes 196608 | tf_op jit(solution)/shard_map/reduce_scatter | solution.py:253
  7.2 49.5 %collective-permute-start.2 = (f32[2,2,64,2048]{3,2,1,0:T(8,128)}, f32[2,2,64,2048]{3,2,1,0:T(8,128)S(1)}, u32[]{:S(2)}, u32[]{:S(2)}) collective-permute-start(f32[2,2,64,2048]{3,2,1,0:T(8,128)} %param.28), channel_id=1, source_target_pairs={{0,1},{1,2},{2,3},{3,4},{4,5},{5,6},{6,7},{7,8},{8,9},{9,10},{10,1... | collective-permute-start | bytes 6291464 | tf_op jit(solution)/shard_map/ppermute | solution.py:18
  10.6 49.3 %collective-permute-start.3 = (f32[2,2,64,2048]{3,2,1,0:T(8,128)}, f32[2,2,64,2048]{3,2,1,0:T(8,128)}, u32[]{:S(2)}, u32[]{:S(2)}) collective-permute-start(f32[2,2,64,2048]{3,2,1,0:T(8,128)} %param.28), channel_id=1, source_target_pairs={{1,0},{2,1},{3,2},{4,3},{5,4},{6,5},{7,6},{8,7},{9,8},{10,9},{11,1... | collective-permute-start | bytes 6291464 | tf_op jit(solution)/shard_map/ppermute | solution.py:19
  65.8 26.6 %copy-start.1 = (f32[2,128,128]{2,1,0:T(8,128)S(1)}, f32[2,128,128]{2,1,0:T(8,128)}, u32[]{:S(2)}) copy-start(f32[2,128,128]{2,1,0:T(8,128)} %param.29) | copy-start | bytes 393220
  106.8 2.3 collective-permute-start
  123.4 11.3 %collective-permute-start = (f32[1,2,128,128]{3,2,1,0:T(8,128)S(1)}, f32[1,2,128,128]{3,2,1,0:T(8,128)S(1)}, u32[]{:S(2)}, u32[]{:S(2)}) collective-permute-start(f32[1,2,128,128]{3,2,1,0:T(8,128)S(1)} %get-tuple-element.2677), channel_id=1, source_target_pairs={{0,128},{1,129},{2,130},{3,131},{4,132},{5,133},{6,134},{7,135},{8... | collective-permute-start | bytes 393224 | tf_op jit(solution)/shard_map/while/body/eval_jaxpr/ppermute | solution.py:27
  135.6 24.8 %collective-permute-start = (f32[1,2,128,128]{3,2,1,0:T(8,128)S(1)}, f32[1,2,128,128]{3,2,1,0:T(8,128)S(1)}, u32[]{:S(2)}, u32[]{:S(2)}) collective-permute-start(f32[1,2,128,128]{3,2,1,0:T(8,128)S(1)} %get-tuple-element.2677), channel_id=1, source_target_pairs={{0,128},{1,129},{2,130},{3,131},{4,132},{5,133},{6,134},{7,135},{8... | collective-permute-start | bytes 393224 | tf_op jit(solution)/shard_map/while/body/eval_jaxpr/ppermute | solution.py:27
  161.3 3.2 collective-permute-start
  165.4 3.2 collective-permute-start
  169.4 3.2 collective-permute-start
  173.5 3.2 collective-permute-start
  177.6 3.2 collective-permute-start
  181.7 3.2 collective-permute-start
  187.6 22.4 %collective-permute-start.1 = (f32[1,2,128,128]{3,2,1,0:T(8,128)S(1)}, f32[1,2,128,128]{3,2,1,0:T(8,128)S(1)}, u32[]{:S(2)}, u32[]{:S(2)}) collective-permute-start(f32[1,2,128,128]{3,2,1,0:T(8,128)S(1)} %get-tuple-element.2694), channel_id=1, source_target_pairs={{128,0},{129,1},{130,2},{131,3},{132,4},{133,5},{134,6},{135,7},{1... | collective-permute-start | bytes 393224 | tf_op jit(solution)/shard_map/while/body/eval_jaxpr/ppermute | solution.py:27
  230.8 3.2 collective-permute-start.1
  254.8 3.2 collective-permute-start.1
  258.9 3.2 collective-permute-start.1
  263.0 3.2 collective-permute-start.1
  267.1 3.2 collective-permute-start.1
  271.2 3.2 collective-permute-start.1
  275.3 3.2 collective-permute-start.1
  279.4 3.2 collective-permute-start.1
  282.6 0.6 copy-start
  283.3 426.6 %all-gather.3.cloned.1.call-start = ((), (), s32[]{:S(2)}) async-start(), calls=%async_computation.2 | async-start | bytes 8454144 | tf_op jit(solution)/shard_map/all_gather | solution.py:101
  543.1 3.5 copy-start.2
  652.8 51.8 %collective-permute-start.4 = (f32[2,2,64,2048]{3,2,1,0:T(8,128)S(1)}, f32[2,2,64,2048]{3,2,1,0:T(8,128)S(1)}, u32[]{:S(2)}, u32[]{:S(2)}) collective-permute-start(f32[2,2,64,2048]{3,2,1,0:T(8,128)S(1)} %get-tuple-element.2463), channel_id=1, source_target_pairs={{0,1},{1,2},{2,3},{3,4},{4,5},{5,6},{6,7},{7,8},{8,9},{9,10},{10,1... | collective-permute-start | bytes 6291464 | tf_op jit(solution)/shard_map/ppermute | solution.py:18
  656.5 49.9 %collective-permute-start.5 = (f32[2,2,64,2048]{3,2,1,0:T(8,128)S(1)}, f32[2,2,64,2048]{3,2,1,0:T(8,128)S(1)}, u32[]{:S(2)}, u32[]{:S(2)}) collective-permute-start(f32[2,2,64,2048]{3,2,1,0:T(8,128)S(1)} %get-tuple-element.2464), channel_id=1, source_target_pairs={{1,0},{2,1},{3,2},{4,3},{5,4},{6,5},{7,6},{8,7},{9,8},{10,9},{11,1... | collective-permute-start | bytes 6291464 | tf_op jit(solution)/shard_map/ppermute | solution.py:19
Sparse Core Ops, SparseCore 0:
  283.4 259.5 reduce-scatter.1
  546.6 125.2 all-gather.2
